TPU v7x, 32 devices: a whole 2x2x4 slice. The times are simulated.
32 devices in a mesh: expert: 8 (over z, y), tensor: 4 (over x, core).
Axes of the slice: x: 2, y: 2, z: 4, core: 2. Of those that a mesh axis runs over, the one named last changes fastest.
Arguments:
- tokens: bfloat16 [1024, 7168], P('expert', 'tensor'), may hold values from -6 to 6
- out_grad: bfloat16 [1024, 7168], P('expert', 'tensor'), may hold values from -1.5 to 1.5
- expert_ids: int32 [1024, 2], P('expert'), may hold values from 0 to 7, all different within a row; in each aligned block of 128 rows (0 to 127, 128 to 255, ...) at most 48 rows name the same one
- gate_values: bfloat16 [1024, 2], P('expert'), may hold values from 0.099609375 to 1
- w_gate: bfloat16 [8, 7168, 1024], P('expert', None, 'tensor'), may hold values from -0.0625 to 0.0625
- w_up: bfloat16 [8, 7168, 1024], P('expert', None, 'tensor'), may hold values from -0.0625 to 0.0625
- w_down: bfloat16 [8, 1024, 7168], P('expert', 'tensor'), may hold values from -0.1875 to 0.1875
Outputs:
- d_tokens: bfloat16 [1024, 7168], P('expert', 'tensor')
- d_gates: float32 [1024, 2], P('expert')
Inputs may be any that keep to these rules, and one draw needn't show every extreme that they name: `expert_ids`: each row names 2 different experts. Among the 128 rows held at one index along `expert` (one aligned block) no expert is named by more than 48 rows, and in some such block one expert is named by exactly 48.
All inputs are finite; a program needn't handle non-finite values.
Results may differ from a plain program's by a relative error of at most 0.0049.
Values may be sent and summed in bfloat16 or wider, within the bound.
A program may use at most 128 MiB of HBM per device.

v0:
```python
import jax
import jax.numpy as jnp
from jax import lax
from jax.sharding import PartitionSpec as P


def local(tokens, out_grad, expert_ids, gate_values, w_gate, w_up, w_down):
    n_experts = lax.axis_size("expert")
    tok_rows, quarter = tokens.shape
    top_count = expert_ids.shape[1]
    most_slots = 3 * tok_rows * top_count // (2 * n_experts)
    slot_count = n_experts * most_slots
    flat_ids = expert_ids.reshape(-1)
    onehot = (flat_ids[:, None] == jnp.arange(n_experts, dtype=jnp.int32)[None, :]).astype(
        jnp.int32
    )
    before = jnp.cumsum(onehot, axis=0) - onehot
    rank = jnp.sum(before * onehot, axis=1)
    slot_of = (flat_ids * most_slots + rank).reshape(tok_rows, top_count)
    matches = slot_of[None, :, :] == jnp.arange(slot_count, dtype=jnp.int32)[:, None, None]
    chooser = jnp.any(matches, axis=2).astype(jnp.bfloat16)
    send_x = jnp.dot(chooser, tokens, preferred_element_type=jnp.float32).astype(jnp.bfloat16)
    send_dy = jnp.dot(chooser, out_grad, preferred_element_type=jnp.float32).astype(jnp.bfloat16)
    gate_wide = gate_values.astype(jnp.float32)[None, :, :]
    send_g = jnp.sum(jnp.where(matches, gate_wide, 0.0), axis=(1, 2)).astype(jnp.bfloat16)
    recv_x, recv_dy, recv_g = (
        lax.all_to_all(
            send_x.reshape(n_experts, most_slots, quarter),
            "expert",
            split_axis=0,
            concat_axis=0,
            tiled=True,
        ),
        lax.all_to_all(
            send_dy.reshape(n_experts, most_slots, quarter),
            "expert",
            split_axis=0,
            concat_axis=0,
            tiled=True,
        ),
        lax.all_to_all(
            send_g.reshape(n_experts, most_slots), "expert", split_axis=0, concat_axis=0, tiled=True
        ),
    )
    rows_x = recv_x.reshape(slot_count, quarter)
    rows_dy = recv_dy.reshape(slot_count, quarter)
    gate_mat = w_gate[0]
    up_mat = w_up[0]
    down_mat = w_down[0]
    piece_x = lax.all_gather(rows_x, "tensor", axis=1, tiled=True)
    piece_dy = lax.all_gather(rows_dy, "tensor", axis=1, tiled=True)
    pre_sum = jnp.dot(piece_x, gate_mat, preferred_element_type=jnp.float32)
    up_sum = jnp.dot(piece_x, up_mat, preferred_element_type=jnp.float32)
    grad_sum = lax.dot_general(
        piece_dy, down_mat, (((1,), (1,)), ((), ())), preferred_element_type=jnp.float32
    )
    sigma = jax.nn.sigmoid(pre_sum)
    active = pre_sum * sigma
    partial_grad = jnp.sum(active * up_sum * grad_sum, axis=1)
    weight_g = recv_g.reshape(slot_count).astype(jnp.float32)
    scaled = weight_g[:, None] * grad_sum
    grad_up = (scaled * active).astype(jnp.bfloat16)
    grad_pre = (scaled * up_sum * sigma * (1.0 + pre_sum * (1.0 - sigma))).astype(jnp.bfloat16)
    contrib = lax.dot_general(
        grad_pre, gate_mat, (((1,), (1,)), ((), ())), preferred_element_type=jnp.float32
    )
    contrib = contrib + lax.dot_general(
        grad_up, up_mat, (((1,), (1,)), ((), ())), preferred_element_type=jnp.float32
    )
    slot_grad = lax.psum(partial_grad, "tensor")
    returned, returned_grad = (
        lax.all_to_all(
            contrib.reshape(n_experts, most_slots, contrib.shape[1]),
            "expert",
            split_axis=0,
            concat_axis=0,
            tiled=True,
        ),
        lax.all_to_all(
            slot_grad.reshape(n_experts, most_slots),
            "expert",
            split_axis=0,
            concat_axis=0,
            tiled=True,
        ),
    )
    slot_rows = returned.reshape(slot_count, contrib.shape[1])
    combined = jnp.sum(jnp.take(slot_rows, slot_of, axis=0), axis=1)
    d_tokens = lax.psum_scatter(combined, "tensor", scatter_dimension=1, tiled=True).astype(
        jnp.bfloat16
    )
    d_gates = jnp.take(returned_grad.reshape(slot_count), slot_of, axis=0)
    return (d_tokens, d_gates)


def solution(mesh):
    placed = (
        P("expert", "tensor"),
        P("expert", "tensor"),
        P("expert", None),
        P("expert", None),
        P("expert", None, "tensor"),
        P("expert", None, "tensor"),
        P("expert", "tensor", None),
    )
    return jax.shard_map(
        local,
        mesh=mesh,
        in_specs=placed,
        out_specs=(P("expert", "tensor"), P("expert", None)),
        check_vma=False,
    )
```

profile of v0, /device:TPU:0, one launch (start us, length us, event | category | flops | bytes accessed | tf_op | source)
XLA Modules:
  0.0 491.3 jit_solution(14696424435222848767)
XLA Ops:
  7.2 0.0 copy-start
  7.2 0.0 copy-start.4
  7.2 0.0 all-gather.5.cloned.1.call-start
  7.2 0.9 copy.32
  8.1 0.1 eq.42
  8.2 0.1 eq.38
  8.4 0.6 reduce-window.6
  9.0 0.2 slice_reduce_fusion
  9.2 0.1 fusion.16
  9.3 0.1 reduce_sum.39
  9.5 0.1 copy.34
  9.5 0.7 compare_select_fusion
  10.3 0.0 copy-done
  10.3 0.5 convolution_convert_fusion
  10.8 40.6 %all_to_all.30 = bf16[8,48,1792]{2,1,0:T(8,128)(2,1)} all-to-all(bf16[8,48,1792]{2,1,0:T(8,128)(2,1)S(1)} %bitcast.40), channel_id=1, replica_groups=mesh['expert'=8,'tensor'=4] {'expert'}, dimensions={0} | all-to-all | bytes 2752512 | tf_op jit(solution)/shard_map/all_to_all | solution.py:27
  51.4 0.0 copy-start.6
  51.4 0.0 all-gather.5.cloned.1.call-update
  51.4 0.0 all-gather.3.cloned.1.call-start
  51.5 0.0 copy-done.4
  51.5 0.5 convolution_convert_fusion.1
  52.0 36.1 %all_to_all.31 = bf16[8,48,1792]{2,1,0:T(8,128)(2,1)} all-to-all(bf16[8,48,1792]{2,1,0:T(8,128)(2,1)S(1)} %bitcast.39), channel_id=1, replica_groups=mesh['expert'=8,'tensor'=4] {'expert'}, dimensions={0} | all-to-all | bytes 2752512 | tf_op jit(solution)/shard_map/all_to_all | solution.py:34
  88.1 0.0 all-gather.3.cloned.1.call-update
  88.2 0.0 copy-done.6
  88.2 0.1 select_reduce_fusion.1
  88.3 0.1 convert_element_type.63
  88.4 9.2 %all_to_all.32 = bf16[8,1,48]{2,1,0:T(2,128)(2,1)S(1)} all-to-all(bf16[8,1,48]{2,1,0:T(2,128)(2,1)S(1)} %convert_element_type.63), channel_id=1, replica_groups=mesh['expert'=8,'tensor'=4] {'expert'}, dimensions={0} | all-to-all | bytes 1536 | tf_op jit(solution)/shard_map/all_to_all | solution.py:41
  97.6 0.1 reshape.94
  97.7 0.0 copy-start.2
  97.7 0.0 copy-start.5
  97.7 6.8 %fusion.2 = f32[384,256]{0,1:T(8,128)S(1)} fusion(bf16[384,7168]{1,0:T(8,128)(2,1)} %all-gather.5.cloned.1.call-done, bf16[1,7168,256]{2,1,0:T(8,128)(2,1)} %param.11), kind=kOutput, calls=%fused_computation.6 | convolution fusion | flops 1409286144 | bytes 9568256 | tf_op jit(solution)/shard_map/dot_general | solution.py:52
  104.5 0.0 copy-done.2
  104.5 1.4 copy-done.5
  105.9 2.1 fusion.5
  108.0 27.4 %all-gather.3.cloned.1.call-done = bf16[384,7168]{1,0:T(8,128)(2,1)} async-done(((bf16[384,1792]{1,0:T(8,128)(2,1)}), bf16[384,7168]{1,0:T(8,128)(2,1)}) %all-gather.3.cloned.1.call-update) | async-done | bytes 5505040 | tf_op jit(solution)/shard_map/all_gather | solution.py:51
  135.4 5.8 %multiply_reduce_fusion = (f32[384]{0:T(512)S(1)}, f32[384,256]{0,1:T(8,128)S(1)}) fusion(f32[384,256]{0,1:T(8,128)S(1)} %fusion.5, f32[384,256]{0,1:T(8,128)S(1)} %fusion.2, bf16[384,7168]{1,0:T(8,128)(2,1)} %all-gather.3.cloned.1.call-done, bf16[1,256,7168]{2,1,0:T(8,128)(2,1)} %param.13), kind=kOutput, calls=%fused_computation.15 | convolution fusion | flops 1409973888 | bytes 10356224 | tf_op jit(solution)/shard_map/dot_general | solution.py:54
  141.2 0.1 all_to_all.23
  141.3 6.5 %psum.7 = f32[8,1,48]{2,1,0:T(1,128)} all-reduce(f32[8,1,48]{2,1,0:T(1,128)S(1)} %all_to_all.23), channel_id=1, replica_groups=mesh['expert'=8,'tensor'=4] {'tensor'}, use_global_device_ids=true, to_apply=%region_8.9 | all-reduce | flops 384 | bytes 3072 | tf_op jit(solution)/shard_map/psum | solution.py:70
  147.8 5.7 %all-to-all-start.4 = ((f32[8,1,48]{2,1,0:T(1,128)}), f32[8,1,48]{2,1,0:T(1,128)S(1)}, u32[]{:S(2)}, u32[]{:S(2)}) async-start(f32[8,1,48]{2,1,0:T(1,128)} %psum.7), calls=%async_computation.5 | async-start | bytes 8192 | tf_op jit(solution)/shard_map/all_to_all | solution.py:79
  153.4 0.0 copy-start.3
  153.4 4.0 fusion
  157.4 0.0 copy-done.3
  157.4 5.7 %convolution_add_fusion = f32[384,7168]{1,0:T(8,128)} fusion(f32[384,7168]{1,0:T(8,128)S(1)} %fusion, bf16[1,7168,256]{2,1,0:T(8,128)(2,1)S(1)} %copy-done.3, f32[384,256]{0,1:T(8,128)S(1)} %get-tuple-element.13, f32[384]{0:T(512)S(1)} %reshape.94, f32[384,256]{0,1:T(8,128)S(1)} %fusion.2), kind=kOutput, calls=%fused_computation.2 | convolution fusion | flops 1412726784 | bytes 26478080 | tf_op jit(solution)/shard_map/dot_general | solution.py:67
  163.1 0.0 all-to-all-done.4
  163.1 6.0 %all-to-all-start.3 = ((f32[8,48,7168]{2,1,0:T(8,128)}), f32[8,48,7168]{2,1,0:T(8,128)}, u32[]{:S(2)}, u32[]{:S(2)}) async-start(f32[8,48,7168]{2,1,0:T(8,128)} %bitcast.36), calls=%async_computation.3 | async-start | bytes 22020096 | tf_op jit(solution)/shard_map/all_to_all | solution.py:72
  169.1 0.0 reduce-scatter.2.cloned.1.call-start
  169.2 0.1 copy.37
  169.3 0.1 reshape.97
  169.4 0.5 broadcast.53
  170.0 0.7 reduce.9
  170.6 0.1 reshape.93
  170.7 1.9 gather_fusion.1
  172.7 0.1 reshape.104
  172.8 0.1 copy.38
  172.9 0.6 broadcast_select_fusion
  173.5 0.1 copy.35
  173.6 233.9 %all-to-all-done.3 = f32[8,48,7168]{2,1,0:T(8,128)} async-done(((f32[8,48,7168]{2,1,0:T(8,128)}), f32[8,48,7168]{2,1,0:T(8,128)}, u32[]{:S(2)}, u32[]{:S(2)}) %all-to-all-start.3) | async-done | bytes 11010080 | tf_op jit(solution)/shard_map/all_to_all | solution.py:72
  407.5 13.0 %gather_fusion = f32[256,7168]{1,0:T(8,128)} fusion(f32[384,7168]{1,0:T(8,128)} %bitcast.10, s32[1024]{0:T(1024)S(1)} %pad_clamp_fusion), kind=kCustom, calls=%fused_computation | custom fusion | bytes 14681088 | tf_op jit(solution)/shard_map/jit(_take)/gather | solution.py:88
  420.5 9.3 %reshape.96 = f32[128,2,7168]{2,1,0:T(2,128)} reshape(f32[256,7168]{1,0:T(8,128)} %gather_fusion) | data formatting | bytes 14680064 | tf_op jit(solution)/shard_map/jit(_take)/gather | solution.py:88
  429.8 0.0 copy-start.1
  429.8 13.4 %select_reduce_fusion = f32[128,7168]{1,0:T(8,128)} fusion(f32[128,2,7168]{2,1,0:T(2,128)} %reshape.96, pred[128,2]{1,0:T(8,128)(4,1)S(1)} %copy.35), kind=kLoop, calls=%fused_computation.3 | loop fusion | flops 2752512 | bytes 11010304 | tf_op jit(solution)/shard_map/reduce_sum | solution.py:88
  443.2 0.0 reduce-scatter.2.cloned.1.call-update
  443.2 39.5 %reduce-scatter.2.cloned.1.call-done = f32[128,1792]{1,0:T(8,128)} async-done(((f32[128,7168]{1,0:T(8,128)}), f32[128,1792]{1,0:T(8,128)}) %reduce-scatter.2.cloned.1.call-update) | async-done | bytes 917520 | tf_op jit(solution)/shard_map/reduce_scatter | solution.py:89
  482.8 2.0 convert_element_type.61
  484.8 0.0 copy-done.1
  (8 shorter events, 0.1 us)
Async XLA Ops:
  7.2 3.1 copy-start
  7.2 44.3 %copy-start.4 = (bf16[128,1792]{1,0:T(8,128)(2,1)S(1)}, bf16[128,1792]{1,0:T(8,128)(2,1)}, u32[]{:S(2)}) copy-start(bf16[128,1792]{1,0:T(8,128)(2,1)} %param.8) | copy-start | bytes 1376260
  7.2 90.5 %all-gather.5.cloned.1.call-start = ((), (), s32[]{:S(2)}) async-start(), calls=%async_computation.7 | async-start | bytes 6881280 | tf_op jit(solution)/shard_map/all_gather | solution.py:50
  51.4 36.7 %copy-start.6 = (bf16[128,2]{0,1:T(2,128)(2,1)S(1)}, bf16[128,2]{0,1:T(2,128)(2,1)}, u32[]{:S(2)}) copy-start(bf16[128,2]{0,1:T(2,128)(2,1)} %param.10) | copy-start | bytes 1540
  51.4 84.0 %all-gather.3.cloned.1.call-start = ((), (), s32[]{:S(2)}) async-start(), calls=%async_computation.6 | async-start | bytes 6881280 | tf_op jit(solution)/shard_map/all_gather | solution.py:51
  97.7 6.8 %copy-start.2 = (bf16[1,7168,256]{2,1,0:T(8,128)(2,1)S(1)}, bf16[1,7168,256]{2,1,0:T(8,128)(2,1)}, u32[]{:S(2)}) copy-start(bf16[1,7168,256]{2,1,0:T(8,128)(2,1)} %param.12) | copy-start | bytes 11010052
  97.7 8.2 %copy-start.5 = (bf16[384,7168]{1,0:T(8,128)(2,1)S(1)}, bf16[384,7168]{1,0:T(8,128)(2,1)}, u32[]{:S(2)}) copy-start(bf16[384,7168]{1,0:T(8,128)(2,1)} %all-gather.5.cloned.1.call-done) | copy-start | bytes 16515076
  147.8 15.4 %all-to-all-start.4 = ((f32[8,1,48]{2,1,0:T(1,128)}), f32[8,1,48]{2,1,0:T(1,128)S(1)}, u32[]{:S(2)}, u32[]{:S(2)}) async-start(f32[8,1,48]{2,1,0:T(1,128)} %psum.7), calls=%async_computation.5 | async-start | bytes 8192 | tf_op jit(solution)/shard_map/all_to_all | solution.py:79
  153.4 4.0 copy-start.3
  163.1 244.4 %all-to-all-start.3 = ((f32[8,48,7168]{2,1,0:T(8,128)}), f32[8,48,7168]{2,1,0:T(8,128)}, u32[]{:S(2)}, u32[]{:S(2)}) async-start(f32[8,48,7168]{2,1,0:T(8,128)} %bitcast.36), calls=%async_computation.3 | async-start | bytes 22020096 | tf_op jit(solution)/shard_map/all_to_all | solution.py:72
  169.1 313.7 %reduce-scatter.2.cloned.1.call-start = ((), (), s32[]{:S(2)}) async-start(), calls=%async_computation.8 | async-start | bytes 4587520 | tf_op jit(solution)/shard_map/reduce_scatter | solution.py:89
  429.8 55.0 %copy-start.1 = (bf16[128,1792]{1,0:T(8,128)(2,1)S(1)}, bf16[128,1792]{1,0:T(8,128)(2,1)}, u32[]{:S(2)}) copy-start(bf16[128,1792]{1,0:T(8,128)(2,1)} %param.7) | copy-start | bytes 1376260
Sparse Core Ops, SparseCore 0:
  51.6 40.2 all-gather.4
  93.5 41.9 all-gather.2
  443.4 39.3 reduce-scatter.1
where the time goes:
time: 492 us; the launch traced here: 491 us
  waiting for transfers between devices  301 us (61%)
  blocking collectives  92.4 us (19%)
  local copies, waits for them, and re-layouts  28.6 us (6%)
  matrix products  25.3 us (5%)
  other arithmetic  18.3 us (4%)
  between operations  13.9 us (3%)
  starting transfers between devices  11.8 us (2%)
    all_to_all x1, waiting for transfers between devices, local(): lax.all_to_all(contrib.reshape(n_experts, most_slots, contrib.shape[1]),...  234 us
    all_to_all x1, blocking collectives, local(): lax.all_to_all(send_x.reshape(n_experts, most_slots, quarter), 'expert',...  40.6 us
    reduce_scatter x1, waiting for transfers between devices, local(): lax.psum_scatter(combined, 'tensor', scatter_dimension=1, tiled=True)  39.5 us
    all_to_all x1, blocking collectives, local(): lax.all_to_all(send_dy.reshape(n_experts, most_slots, quarter), 'expert',...  36.1 us
    all_gather x1, waiting for transfers between devices, local(): piece_dy = lax.all_gather(rows_dy, 'tensor', axis=1, tiled=True)  27.4 us
    gather x2, local copies, waits for them, and re-layouts, local(): combined = jnp.sum(jnp.take(slot_rows, slot_of, axis=0), axis=1)  22.2 us
    reduce_sum x1, other arithmetic, local(): combined = jnp.sum(jnp.take(slot_rows, slot_of, axis=0), axis=1)  13.4 us
  transfers between devices with their start and end apart: 5, of which 3 were waited for; matrix products, arithmetic and copies ran while one was open for 5% of the time, Pallas kernels for 0%

commit v1 on v0

--- a/solution.py
+++ b/solution.py
@@ -2,6 +2,7 @@
 import jax.numpy as jnp
 from jax import lax
 from jax.sharding import PartitionSpec as P
+from jax.lax import all_gather
 
 
 def local(tokens, out_grad, expert_ids, gate_values, w_gate, w_up, w_down):
@@ -47,8 +48,9 @@
     gate_mat = w_gate[0]
     up_mat = w_up[0]
     down_mat = w_down[0]
-    piece_x = lax.all_gather(rows_x, "tensor", axis=1, tiled=True)
-    piece_dy = lax.all_gather(rows_dy, "tensor", axis=1, tiled=True)
+    row_out = jnp.concatenate([rows_x, rows_dy], axis=0)
+    reply = all_gather(row_out, "tensor", axis=1, tiled=True)
+    piece_x, piece_dy = jnp.split(reply, [rows_x.shape[0]], axis=0)
     pre_sum = jnp.dot(piece_x, gate_mat, preferred_element_type=jnp.float32)
     up_sum = jnp.dot(piece_x, up_mat, preferred_element_type=jnp.float32)
     grad_sum = lax.dot_general(

time: 492 us -> 527 us (1.071)
  waiting for transfers between devices: 301 us -> 367 us
  blocking collectives: 92.4 us -> 52.7 us
  starting transfers between devices: 11.8 us -> 19 us
    all_to_all x1 -> x0, blocking collectives: 40.6 us -> none  [local(): lax.all_to_all(send_x.reshape(n_experts, most_slots, quarter), 'expert',...]
    all_gather x2 -> x1, waiting for transfers between devices: 27.4 us -> 62.1 us  [local(): reply = all_gather(row_out, 'tensor', axis=1, tiled=True)]
    all_to_all x0 -> x1, waiting for transfers between devices: none -> 31.2 us  [local(): lax.all_to_all(send_x.reshape(n_experts, most_slots, quarter), 'expert',...]
    all_to_all x0 -> x1, starting transfers between devices: none -> 7.28 us  [local(): lax.all_to_all(send_x.reshape(n_experts, most_slots, quarter), 'expert',...]
  transfers between devices with their start and end apart: 5 -> 5, of which waited for: 3 -> 4; matrix products, arithmetic and copies ran while one was open for 5% -> 3% of each run, Pallas kernels for 0% -> 0%
where the time goes in v1:
time: 527 us; the launch traced here: 526 us
  waiting for transfers between devices  367 us (70%)
  blocking collectives  52.7 us (10%)
  local copies, waits for them, and re-layouts  27.2 us (5%)
  matrix products  25.7 us (5%)
  other arithmetic  20.1 us (4%)
  starting transfers between devices  19 us (4%)
  between operations  14.3 us (3%)
    all_to_all x1, waiting for transfers between devices, local(): lax.all_to_all(contrib.reshape(n_experts, most_slots, contrib.shape[1]),...  234 us
    all_gather x1, waiting for transfers between devices, local(): reply = all_gather(row_out, 'tensor', axis=1, tiled=True)  62.1 us
    reduce_scatter x1, waiting for transfers between devices, local(): lax.psum_scatter(combined, 'tensor', scatter_dimension=1, tiled=True)  39.5 us
    all_to_all x1, blocking collectives, local(): lax.all_to_all(send_dy.reshape(n_experts, most_slots, quarter), 'expert',...  37 us
    all_to_all x1, waiting for transfers between devices, local(): lax.all_to_all(send_x.reshape(n_experts, most_slots, quarter), 'expert',...  31.2 us
    gather x2, local copies, waits for them, and re-layouts, local(): combined = jnp.sum(jnp.take(slot_rows, slot_of, axis=0), axis=1)  22.2 us
    reduce_sum x1, other arithmetic, local(): combined = jnp.sum(jnp.take(slot_rows, slot_of, axis=0), axis=1)  13.4 us
  transfers between devices with their start and end apart: 5, of which 4 were waited for; matrix products, arithmetic and copies ran while one was open for 3% of the time, Pallas kernels for 0%

profile of v1, /device:TPU:0, one launch (start us, length us, event | category | flops | bytes accessed | tf_op | source)
XLA Modules:
  0.0 525.9 jit_solution(10138759243282469262)
XLA Ops:
  7.2 0.0 copy-start
  7.2 0.8 copy.32
  8.0 0.1 eq.42
  8.2 0.1 eq.38
  8.3 0.6 reduce-window.6
  8.9 0.2 slice_reduce_fusion
  9.2 0.1 fusion.19
  9.3 0.1 reduce_sum.39
  9.4 0.1 copy.34
  9.5 0.7 compare_select_fusion
  10.2 0.0 copy-done
  10.2 1.6 convolution_convert_fusion.1
  11.8 7.3 %all-to-all-start.1 = ((bf16[8,48,1792]{2,1,0:T(8,128)(2,1)}), bf16[8,48,1792]{2,1,0:T(8,128)(2,1)S(1)}, u32[]{:S(2)}, u32[]{:S(2)}) async-start(bf16[8,48,1792]{2,1,0:T(8,128)(2,1)} %bitcast.2), calls=%async_computation.1 | async-start | bytes 2752512 | tf_op jit(solution)/shard_map/all_to_all | solution.py:28
  19.1 0.0 all-gather.2.cloned.1.call-start
  19.1 1.5 convolution_convert_fusion
  20.7 31.2 %all-to-all-done.1 = bf16[8,48,1792]{2,1,0:T(8,128)(2,1)S(1)} async-done(((bf16[8,48,1792]{2,1,0:T(8,128)(2,1)}), bf16[8,48,1792]{2,1,0:T(8,128)(2,1)S(1)}, u32[]{:S(2)}, u32[]{:S(2)}) %all-to-all-start.1) | async-done | bytes 1376288 | tf_op jit(solution)/shard_map/all_to_all | solution.py:28
  51.9 37.0 %all_to_all.30 = bf16[8,48,1792]{2,1,0:T(8,128)(2,1)S(1)} all-to-all(bf16[8,48,1792]{2,1,0:T(8,128)(2,1)S(1)} %bitcast.35), channel_id=1, replica_groups=mesh['expert'=8,'tensor'=4] {'expert'}, dimensions={0} | all-to-all | bytes 2752512 | tf_op jit(solution)/shard_map/all_to_all | solution.py:35
  88.9 0.0 copy-start.5
  88.9 1.8 pad_maximum_fusion
  90.7 0.0 all-gather.2.cloned.1.call-update
  90.7 0.0 copy-done.5
  90.7 0.1 select_reduce_fusion.1
  90.9 0.1 convert_element_type.63
  91.0 9.3 %all_to_all.31 = bf16[8,1,48]{2,1,0:T(2,128)(2,1)S(1)} all-to-all(bf16[8,1,48]{2,1,0:T(2,128)(2,1)S(1)} %convert_element_type.63), channel_id=1, replica_groups=mesh['expert'=8,'tensor'=4] {'expert'}, dimensions={0} | all-to-all | bytes 1536 | tf_op jit(solution)/shard_map/all_to_all | solution.py:42
  100.2 0.1 reshape.94
  100.3 62.1 %all-gather.2.cloned.1.call-done = bf16[768,7168]{1,0:T(8,128)(2,1)} async-done(((bf16[768,1792]{1,0:T(8,128)(2,1)}), bf16[768,7168]{1,0:T(8,128)(2,1)}) %all-gather.2.cloned.1.call-update) | async-done | bytes 11010064 | tf_op jit(solution)/shard_map/all_gather | solution.py:52
  162.5 0.0 copy-start.2
  162.5 5.9 %fusion.2 = f32[384,256]{0,1:T(8,128)S(1)} fusion(bf16[768,7168]{1,0:T(8,128)(2,1)} %all-gather.2.cloned.1.call-done, bf16[1,7168,256]{2,1,0:T(8,128)(2,1)} %param.11), kind=kOutput, calls=%fused_computation.6 | convolution fusion | flops 1409286144 | bytes 9568256 | tf_op jit(solution)/shard_map/dot_general | solution.py:54
  168.4 0.0 copy-done.2
  168.4 0.0 slice-start.2
  168.4 0.0 copy-start.4
  168.4 4.9 fusion.4
  173.4 0.0 slice-done
  173.4 0.0 slice-done.1
  173.4 0.0 slice-done.2
  173.4 0.0 copy-done.4
  173.4 2.1 multiply_reduce_fusion
  175.5 0.1 all_to_all.23
  175.6 6.5 %psum.7 = f32[8,1,48]{2,1,0:T(1,128)} all-reduce(f32[8,1,48]{2,1,0:T(1,128)S(1)} %all_to_all.23), channel_id=1, replica_groups=mesh['expert'=8,'tensor'=4] {'tensor'}, use_global_device_ids=true, to_apply=%region_8.9 | all-reduce | flops 384 | bytes 3072 | tf_op jit(solution)/shard_map/psum | solution.py:72
  182.1 5.7 %all-to-all-start.4 = ((f32[8,1,48]{2,1,0:T(1,128)}), f32[8,1,48]{2,1,0:T(1,128)S(1)}, u32[]{:S(2)}, u32[]{:S(2)}) async-start(f32[8,1,48]{2,1,0:T(1,128)} %psum.7), calls=%async_computation.5 | async-start | bytes 8192 | tf_op jit(solution)/shard_map/all_to_all | solution.py:81
  187.8 4.0 fusion.6
  191.7 0.0 copy-done.3
  191.7 5.7 %convolution_add_fusion = f32[384,7168]{1,0:T(8,128)} fusion(f32[384,7168]{1,0:T(8,128)S(1)} %fusion.6, bf16[1,7168,256]{2,1,0:T(8,128)(2,1)S(1)} %copy-done.3, f32[384,256]{0,1:T(8,128)S(1)} %get-tuple-element.13, f32[384]{0:T(512)S(1)} %reshape.94, f32[384,256]{0,1:T(8,128)S(1)} %fusion.2), kind=kOutput, calls=%fused_computation.2 | convolution fusion | flops 1412726784 | bytes 26478080 | tf_op jit(solution)/shard_map/dot_general | solution.py:69
  197.5 0.0 all-to-all-done.4
  197.5 6.0 %all-to-all-start.3 = ((f32[8,48,7168]{2,1,0:T(8,128)}), f32[8,48,7168]{2,1,0:T(8,128)}, u32[]{:S(2)}, u32[]{:S(2)}) async-start(f32[8,48,7168]{2,1,0:T(8,128)} %bitcast.33), calls=%async_computation.3 | async-start | bytes 22020096 | tf_op jit(solution)/shard_map/all_to_all | solution.py:74
  203.5 0.0 reduce-scatter.2.cloned.1.call-start
  203.5 0.1 copy.37
  203.6 0.1 reshape.97
  203.8 0.5 broadcast.53
  204.3 0.7 reduce.9
  204.9 0.1 reshape.93
  205.0 1.9 gather_fusion.1
  207.0 0.1 reshape.104
  207.1 0.1 copy.38
  207.2 0.6 broadcast_select_fusion
  207.8 0.1 copy.35
  207.9 234.0 %all-to-all-done.3 = f32[8,48,7168]{2,1,0:T(8,128)} async-done(((f32[8,48,7168]{2,1,0:T(8,128)}), f32[8,48,7168]{2,1,0:T(8,128)}, u32[]{:S(2)}, u32[]{:S(2)}) %all-to-all-start.3) | async-done | bytes 11010080 | tf_op jit(solution)/shard_map/all_to_all | solution.py:74
  441.9 13.0 %gather_fusion = f32[256,7168]{1,0:T(8,128)} fusion(f32[384,7168]{1,0:T(8,128)} %bitcast.10, s32[1024]{0:T(1024)S(1)} %pad_clamp_fusion), kind=kCustom, calls=%fused_computation | custom fusion | bytes 14681088 | tf_op jit(solution)/shard_map/jit(_take)/gather | solution.py:90
  454.8 9.3 %reshape.96 = f32[128,2,7168]{2,1,0:T(2,128)} reshape(f32[256,7168]{1,0:T(8,128)} %gather_fusion) | data formatting | bytes 14680064 | tf_op jit(solution)/shard_map/jit(_take)/gather | solution.py:90
  464.1 13.4 %select_reduce_fusion = f32[128,7168]{1,0:T(8,128)} fusion(f32[128,2,7168]{2,1,0:T(2,128)} %reshape.96, pred[128,2]{1,0:T(8,128)(4,1)S(1)} %copy.35), kind=kLoop, calls=%fused_computation.3 | loop fusion | flops 2752512 | bytes 11010304 | tf_op jit(solution)/shard_map/reduce_sum | solution.py:90
  477.5 0.0 reduce-scatter.2.cloned.1.call-update
  477.6 39.5 %reduce-scatter.2.cloned.1.call-done = f32[128,1792]{1,0:T(8,128)} async-done(((f32[128,7168]{1,0:T(8,128)}), f32[128,1792]{1,0:T(8,128)}) %reduce-scatter.2.cloned.1.call-update) | async-done | bytes 917520 | tf_op jit(solution)/shard_map/reduce_scatter | solution.py:91
  517.1 2.0 convert_element_type.61
  519.1 0.0 copy-done.1
  (12 shorter events, 0.1 us)
Async XLA Ops:
  7.2 3.1 copy-start
  11.8 40.1 %all-to-all-start.1 = ((bf16[8,48,1792]{2,1,0:T(8,128)(2,1)}), bf16[8,48,1792]{2,1,0:T(8,128)(2,1)S(1)}, u32[]{:S(2)}, u32[]{:S(2)}) async-start(bf16[8,48,1792]{2,1,0:T(8,128)(2,1)} %bitcast.2), calls=%async_computation.1 | async-start | bytes 2752512 | tf_op jit(solution)/shard_map/all_to_all | solution.py:28
  19.1 143.4 %all-gather.2.cloned.1.call-start = ((), (), s32[]{:S(2)}) async-start(), calls=%async_computation.6 | async-start | bytes 13762560 | tf_op jit(solution)/shard_map/all_gather | solution.py:52
  88.9 1.8 copy-start.5
  162.5 5.9 %copy-start.2 = (bf16[1,7168,256]{2,1,0:T(8,128)(2,1)S(1)}, bf16[1,7168,256]{2,1,0:T(8,128)(2,1)}, u32[]{:S(2)}) copy-start(bf16[1,7168,256]{2,1,0:T(8,128)(2,1)} %param.12) | copy-start | bytes 11010052
  162.5 10.9 %slice-start = ((s8[11010048]{0:T(1024)(128)(4,1)}), s8[4194304]{0:T(1024)(128)(4,1)S(1)}, s32[]{:S(2)}) async-start(s8[11010048]{0:T(1024)(128)(4,1)} %bitcast.37), calls=%async_computation.8 | async-start | bytes 8388608
  162.5 10.9 %slice-start.1 = ((s8[11010048]{0:T(1024)(128)(4,1)}), s8[4194304]{0:T(1024)(128)(4,1)S(1)}, s32[]{:S(2)}) async-start(s8[11010048]{0:T(1024)(128)(4,1)} %bitcast.37), calls=%async_computation.9 | async-start | bytes 8388608
  168.4 5.0 slice-start.2
  168.4 5.0 copy-start.4
  182.1 15.4 %all-to-all-start.4 = ((f32[8,1,48]{2,1,0:T(1,128)}), f32[8,1,48]{2,1,0:T(1,128)S(1)}, u32[]{:S(2)}, u32[]{:S(2)}) async-start(f32[8,1,48]{2,1,0:T(1,128)} %psum.7), calls=%async_computation.5 | async-start | bytes 8192 | tf_op jit(solution)/shard_map/all_to_all | solution.py:81
  187.8 4.0 copy-start.3
  197.5 244.4 %all-to-all-start.3 = ((f32[8,48,7168]{2,1,0:T(8,128)}), f32[8,48,7168]{2,1,0:T(8,128)}, u32[]{:S(2)}, u32[]{:S(2)}) async-start(f32[8,48,7168]{2,1,0:T(8,128)} %bitcast.33), calls=%async_computation.3 | async-start | bytes 22020096 | tf_op jit(solution)/shard_map/all_to_all | solution.py:74
  203.5 313.7 %reduce-scatter.2.cloned.1.call-start = ((), (), s32[]{:S(2)}) async-start(), calls=%async_computation.7 | async-start | bytes 4587520 | tf_op jit(solution)/shard_map/reduce_scatter | solution.py:91
  464.1 55.0 %copy-start.1 = (bf16[128,1792]{1,0:T(8,128)(2,1)S(1)}, bf16[128,1792]{1,0:T(8,128)(2,1)}, u32[]{:S(2)}) copy-start(bf16[128,1792]{1,0:T(8,128)(2,1)} %param.7) | copy-start | bytes 1376260
Sparse Core Ops, SparseCore 0:
  90.8 71.5 all-gather.1
  477.7 39.3 reduce-scatter.1
